TPU v7x, 512 devices: a whole 4x8x8 slice. The times are simulated.
512 devices in a mesh: req: 128 (over y, z, core), tp: 4 (over x).
Axes of the slice: x: 4, y: 8, z: 8, core: 2. Of those that a mesh axis runs over, the one named last changes fastest.
Arguments:
- attn_out: bfloat16 [8192, 2048], P('req', 'tp'), may hold values from -6 to 6
- w_out: bfloat16 [2048, 2048], P('tp'), may hold values from -0.125 to 0.125
- residual: bfloat16 [8192, 2048], P('req', 'tp'), may hold values from -6 to 6
- routes: int32 [8192, 6], P('req'), may hold values from 0 to 127, all different within a row; in each aligned block of 64 rows (0 to 63, 64 to 127, ...) at most 6 rows name the same one
- gates: float32 [8192, 6], P('req'), may hold values from 0.05 to 1
- w_gate: bfloat16 [128, 2048, 1024], P('req', None, 'tp'), as said below
- w_up: bfloat16 [128, 2048, 1024], P('req', None, 'tp'), as said below
- w_down: bfloat16 [128, 1024, 2048], P('req', None, 'tp'), as said below
- norm_gain: float32 [2048], P('tp'), may hold values from 0.1 to 1.9
Outputs:
- normed: bfloat16 [8192, 2048], P('req', 'tp')
Inputs may be any that keep to these rules, and one draw needn't show every extreme that they name: `routes`: each row names 6 different slots. In the 64 rows of one index of req no slot is named by more than 6 rows, a bound that some block reaches. `w_gate`: slots 2 e and 2 e + 1 hold the same expert e: their weights are equal. `w_up`: slots 2 e and 2 e + 1 hold the same expert e: their weights are equal. `w_down`: slots 2 e and 2 e + 1 hold the same expert e: their weights are equal.
All inputs are finite; a program needn't handle non-finite values.
Results may differ from a plain program's by a relative error of at most 0.0056.
Values may be sent and summed in bfloat16 or wider, within the bound.
A program may use at most 64 MiB of HBM per device.

v0:
```python
import jax
import jax.numpy as jnp
from jax import lax
from jax.sharding import PartitionSpec as P


def body(attn_out, w_out, residual, routes, gates, w_gate, w_up, w_down, norm_gain):
    row_count = attn_out.shape[0]
    part_width = residual.shape[1]
    full_width = w_out.shape[1]
    route_count = routes.shape[1]
    slot_count = lax.axis_size("req")
    capacity = max(2, min(row_count, 2 * row_count * route_count // slot_count))
    tp_index = lax.axis_index("tp")
    partial_value = jnp.dot(attn_out, w_out, preferred_element_type=jnp.float32)
    own_block = lax.dynamic_slice_in_dim(partial_value, tp_index * part_width, part_width, 1)
    partial_value = lax.dynamic_update_slice_in_dim(
        partial_value, own_block + residual.astype(jnp.float32), tp_index * part_width, 1
    )
    flat_routes = routes.reshape(-1)
    one_hot = (flat_routes[:, None] == jnp.arange(slot_count, dtype=jnp.int32)[None, :]).astype(
        jnp.int32
    )
    position = jnp.sum(one_hot * (jnp.cumsum(one_hot, axis=0) - 1), axis=1)
    dest_index = flat_routes * capacity + position
    row_ids = jnp.repeat(jnp.arange(row_count, dtype=jnp.int32), route_count)
    source_row = jnp.zeros((slot_count * capacity,), jnp.int32).at[dest_index].set(row_ids)
    gate_local = w_gate[0]
    up_local = w_up[0]
    down_local = w_down[0]
    projected = lax.psum(partial_value, "tp")
    own_part = lax.dynamic_slice_in_dim(projected, tp_index * part_width, part_width, 1)
    outgoing = projected.astype(jnp.bfloat16)[source_row].reshape(slot_count, capacity, full_width)
    incoming = lax.all_to_all(outgoing, "req", split_axis=0, concat_axis=0, tiled=True)
    expert_rows = incoming.reshape(slot_count * capacity, full_width)
    gate_act = jnp.dot(expert_rows, gate_local, preferred_element_type=jnp.float32)
    up_act = jnp.dot(expert_rows, up_local, preferred_element_type=jnp.float32)
    hidden = (jax.nn.silu(gate_act) * up_act).astype(jnp.bfloat16)
    expert_out = jnp.dot(
        lax.all_gather(hidden, "tp", axis=1, tiled=True),
        down_local,
        preferred_element_type=jnp.float32,
    )
    expert_out = expert_out.astype(jnp.bfloat16).reshape(slot_count, capacity, down_local.shape[1])
    returned = lax.all_to_all(expert_out, "req", split_axis=0, concat_axis=0, tiled=True)
    picked = returned.reshape(slot_count * capacity, part_width)[dest_index]
    picked = picked.reshape(row_count, route_count, part_width).astype(jnp.float32)
    routed_sum = jnp.sum(picked * gates[:, :, None], axis=1)
    combined = own_part + routed_sum
    square_part = jnp.sum(combined * combined, axis=1)
    square_total = lax.psum(square_part, "tp")
    scale = lax.rsqrt(square_total / full_width + 1e-06)
    return (combined * scale[:, None] * norm_gain[None, :]).astype(jnp.bfloat16)


def solution(mesh):
    placed = (
        P("req", "tp"),
        P("tp", None),
        P("req", "tp"),
        P("req", None),
        P("req", None),
        P("req", None, "tp"),
        P("req", None, "tp"),
        P("req", None, "tp"),
        P("tp"),
    )
    return jax.shard_map(
        body, mesh=mesh, in_specs=placed, out_specs=P("req", "tp"), check_vma=False
    )
```

profile of v0, /device:TPU:8, one launch (start us, length us, event | category | flops | bytes accessed | tf_op | source)
XLA Modules:
  0.0 315.9 jit_solution(1539475655118343820)
XLA Ops:
  6.5 0.0 copy-start
  6.5 0.0 copy-start.3
  6.5 0.0 all-reduce.2.cloned.1.call-start
  6.5 1.6 copy-done
  8.1 1.3 fusion.12
  9.4 0.9 add_dynamic-update-slice_fusion
  10.3 0.0 copy-start.2
  10.3 0.8 copy-done.2
  11.1 0.0 all-reduce.2.cloned.1.call-update
  11.1 0.0 all-gather.2.cloned.1.call-start
  11.2 0.0 copy-done.3
  11.2 0.1 copy.12
  11.3 0.1 eq.29
  11.4 0.1 eq.25
  11.6 0.1 copy.14
  11.7 0.2 fusion.5
  12.0 0.1 add_add_fusion
  12.0 0.1 copy.11
  12.1 0.1 mul.61
  12.3 0.1 reshape.96
  12.4 0.2 fusion.7
  12.7 2.9 scatter_custom_fusion
  15.6 53.9 %all-reduce.2.cloned.1.call-done = f32[64,2048]{1,0:T(8,128)} async-done(((f32[64,2048]{1,0:T(8,128)}), f32[64,2048]{1,0:T(8,128)}) %all-reduce.2.cloned.1.call-update) | async-done | bytes 524304 | tf_op jit(solution)/shard_map/psum | solution.py:31
  69.5 1.1 convert_element_type.27
  70.6 4.3 %gather_fusion = bf16[768,2048]{1,0:T(8,128)(2,1)} fusion(bf16[64,2048]{1,0:T(8,128)(2,1)S(1)} %convert_element_type.27, s32[1024]{0:T(1024)S(1)} %pad_clamp_fusion.1), kind=kCustom, calls=%fused_computation | custom fusion | bytes 6294528 | tf_op jit(solution)/shard_map/gather | solution.py:33
  74.9 6.3 %reshape.71 = bf16[128,6,2048]{2,1,0:T(8,128)(2,1)} reshape(bf16[768,2048]{1,0:T(8,128)(2,1)} %gather_fusion) | data formatting | bytes 6291456 | tf_op jit(solution)/shard_map/reshape | solution.py:33
  81.1 111.0 %all_to_all.10 = bf16[128,6,2048]{2,1,0:T(8,128)(2,1)} all-to-all(bf16[128,6,2048]{2,1,0:T(8,128)(2,1)} %reshape.71), channel_id=1, replica_groups=mesh['req'=128,'tp'=4] {'req'}, dimensions={0} | all-to-all | bytes 6291456 | tf_op jit(solution)/shard_map/all_to_all | solution.py:34
  192.1 6.3 %reshape.72 = bf16[768,2048]{1,0:T(8,128)(2,1)} reshape(bf16[128,6,2048]{2,1,0:T(8,128)(2,1)} %all_to_all.10) | data formatting | bytes 6291456 | tf_op jit(solution)/shard_map/reshape | solution.py:35
  198.4 0.0 copy-start.1
  198.4 0.0 copy-start.6
  198.4 3.3 %fusion.3 = f32[768,256]{1,0:T(8,128)S(1)} fusion(bf16[768,2048]{1,0:T(8,128)(2,1)} %reshape.72, bf16[1,2048,256]{2,1,0:T(8,128)(2,1)} %param.14), kind=kOutput, calls=%fused_computation.8 | convolution fusion | flops 805306368 | bytes 4980736 | tf_op jit(solution)/shard_map/dot_general | solution.py:36
  201.7 0.0 copy-done.1
  201.8 0.1 copy-done.6
  201.9 1.7 fusion
  203.6 0.0 all-gather.2.cloned.1.call-update
  203.6 38.7 %all-gather.2.cloned.1.call-done = bf16[768,1024]{1,0:T(8,128)(2,1)} async-done(((bf16[768,256]{1,0:T(8,128)(2,1)}), bf16[768,1024]{1,0:T(8,128)(2,1)}) %all-gather.2.cloned.1.call-update) | async-done | bytes 1572880 | tf_op jit(solution)/shard_map/all_gather | solution.py:40
  242.3 2.7 convolution_convert_fusion
  245.0 0.0 copy-start.4
  245.0 1.3 reshape.73
  246.3 14.6 %all-to-all-start.1 = ((bf16[128,6,512]{2,1,0:T(8,128)(2,1)}), bf16[128,6,512]{2,1,0:T(8,128)(2,1)}, u32[]{:S(2)}, u32[]{:S(2)}) async-start(bf16[128,6,512]{2,1,0:T(8,128)(2,1)} %reshape.73), calls=%async_computation.1 | async-start | bytes 2097152 | tf_op jit(solution)/shard_map/all_to_all | solution.py:45
  260.9 0.0 copy-done.4
  260.9 0.7 copy.16
  261.6 30.2 %all-to-all-done.1 = bf16[128,6,512]{2,1,0:T(8,128)(2,1)} async-done(((bf16[128,6,512]{2,1,0:T(8,128)(2,1)}), bf16[128,6,512]{2,1,0:T(8,128)(2,1)}, u32[]{:S(2)}, u32[]{:S(2)}) %all-to-all-start.1) | async-done | bytes 786464 | tf_op jit(solution)/shard_map/all_to_all | solution.py:45
  291.9 1.4 reshape.74
  293.2 0.0 copy-start.5
  293.3 2.1 gather_fusion.1
  295.3 0.1 reshape.75
  295.4 1.1 multiply_reduce_fusion
  296.6 1.0 multiply_reduce_fusion.1
  297.6 9.8 %psum.15 = f32[64]{0:T(128)S(1)} all-reduce(f32[64]{0:T(128)S(1)} %multiply_reduce_fusion.1), channel_id=1, replica_groups=mesh['req'=128,'tp'=4] {'tp'}, use_global_device_ids=true, to_apply=%region_7.8 | all-reduce | flops 64 | bytes 512 | tf_op jit(solution)/shard_map/psum | solution.py:51
  307.4 0.0 copy-done.5
  307.4 1.6 multiply_convert_fusion
  (10 shorter events, 0.1 us)
Async XLA Ops:
  6.5 1.6 copy-start
  6.5 4.6 %copy-start.3 = (s32[64,6]{0,1:T(8,128)S(1)}, s32[64,6]{0,1:T(8,128)}, u32[]{:S(2)}) copy-start(s32[64,6]{0,1:T(8,128)} %param.12) | copy-start | bytes 4612
  6.5 63.0 %all-reduce.2.cloned.1.call-start = ((), (), s32[]{:S(2)}) async-start(), calls=%async_computation.2 | async-start | bytes 1048576 | tf_op jit(solution)/shard_map/psum | solution.py:31
  10.3 0.8 copy-start.2
  11.1 231.1 %all-gather.2.cloned.1.call-start = ((), (), s32[]{:S(2)}) async-start(), calls=%async_computation.3 | async-start | bytes 1966080 | tf_op jit(solution)/shard_map/all_gather | solution.py:40
  198.4 3.3 %copy-start.1 = (bf16[768,2048]{1,0:T(8,128)(2,1)S(1)}, bf16[768,2048]{1,0:T(8,128)(2,1)}, u32[]{:S(2)}) copy-start(bf16[768,2048]{1,0:T(8,128)(2,1)} %reshape.72) | copy-start | bytes 9437188
  198.4 3.4 %copy-start.6 = (bf16[1,2048,256]{2,1,0:T(8,128)(2,1)S(1)}, bf16[1,2048,256]{2,1,0:T(8,128)(2,1)}, u32[]{:S(2)}) copy-start(bf16[1,2048,256]{2,1,0:T(8,128)(2,1)} %param.15) | copy-start | bytes 3145732
  245.0 15.9 %copy-start.4 = (f32[64,6]{0,1:T(8,128)S(1)}, f32[64,6]{0,1:T(8,128)}, u32[]{:S(2)}) copy-start(f32[64,6]{0,1:T(8,128)} %param.13) | copy-start | bytes 4612
  246.3 45.6 %all-to-all-start.1 = ((bf16[128,6,512]{2,1,0:T(8,128)(2,1)}), bf16[128,6,512]{2,1,0:T(8,128)(2,1)}, u32[]{:S(2)}, u32[]{:S(2)}) async-start(bf16[128,6,512]{2,1,0:T(8,128)(2,1)} %reshape.73), calls=%async_computation.1 | async-start | bytes 2097152 | tf_op jit(solution)/shard_map/all_to_all | solution.py:45
  293.2 14.2 %copy-start.5 = (f32[512]{0:T(512)S(1)}, f32[512]{0:T(512)}, u32[]{:S(2)}) copy-start(f32[512]{0:T(512)} %param.17) | copy-start | bytes 6148
Sparse Core Ops, SparseCore 0:
  11.3 58.2 all-reduce.1
  203.7 38.5 all-gather.1
where the time goes:
time: 317 us; the launch traced here: 316 us
  waiting for transfers between devices  123 us (39%)
  blocking collectives  121 us (38%)
  local copies, waits for them, and re-layouts  28.7 us (9%)
  starting transfers between devices  14.7 us (5%)
  between operations  13.6 us (4%)
  matrix products  9.02 us (3%)
  other arithmetic  6.31 us (2%)
    all_to_all x1, blocking collectives, body(): lax.all_to_all(outgoing, 'req', split_axis=0, concat_axis=0, tiled=True)  111 us
    psum x1, waiting for transfers between devices, body(): projected = lax.psum(partial_value, 'tp')  53.9 us
    all_gather x1, waiting for transfers between devices, body(): lax.all_gather(hidden, 'tp', axis=1, tiled=True)  38.7 us
    all_to_all x1, waiting for transfers between devices, body(): lax.all_to_all(expert_out, 'req', split_axis=0, concat_axis=0, tiled=True)  30.2 us
    all_to_all x1, starting transfers between devices, body(): lax.all_to_all(expert_out, 'req', split_axis=0, concat_axis=0, tiled=True)  14.6 us
    psum x1, blocking collectives, body(): square_total = lax.psum(square_part, 'tp')  9.8 us
  transfers between devices with their start and end apart: 3, of which 3 were waited for; matrix products, arithmetic and copies ran while one was open for 2% of the time, Pallas kernels for 0%

commit v1 on v0

--- a/solution.py
+++ b/solution.py
@@ -48,7 +48,8 @@
     routed_sum = jnp.sum(picked * gates[:, :, None], axis=1)
     combined = own_part + routed_sum
     square_part = jnp.sum(combined * combined, axis=1)
-    square_total = lax.psum(square_part, "tp")
+    long_array = jax.lax.all_gather(square_part, "tp")
+    square_total = jnp.sum(long_array, axis=0)
     scale = lax.rsqrt(square_total / full_width + 1e-06)
     return (combined * scale[:, None] * norm_gain[None, :]).astype(jnp.bfloat16)
 

time: 317 us -> 317 us (level)
    psum x1 -> x0, blocking collectives: 9.8 us -> none  [body(): square_total = lax.psum(square_part, 'tp')]
    unnamed x0 -> x1, blocking collectives: none -> 9.77 us
where the time goes in v1:
time: 317 us; the launch traced here: 316 us
  waiting for transfers between devices  121 us (38%)
  blocking collectives  121 us (38%)
  local copies, waits for them, and re-layouts  30.3 us (10%)
  starting transfers between devices  14.7 us (5%)
  between operations  14.3 us (5%)
  matrix products  9.02 us (3%)
  other arithmetic  6.34 us (2%)
    all_to_all x1, blocking collectives, body(): lax.all_to_all(outgoing, 'req', split_axis=0, concat_axis=0, tiled=True)  111 us
    psum x1, waiting for transfers between devices, body(): projected = lax.psum(partial_value, 'tp')  53.9 us
    all_gather x1, waiting for transfers between devices, body(): lax.all_gather(hidden, 'tp', axis=1, tiled=True)  38.7 us
    all_to_all x1, waiting for transfers between devices, body(): lax.all_to_all(expert_out, 'req', split_axis=0, concat_axis=0, tiled=True)  28.3 us
    all_to_all x1, starting transfers between devices, body(): lax.all_to_all(expert_out, 'req', split_axis=0, concat_axis=0, tiled=True)  14.6 us
    unnamed x1, blocking collectives  9.77 us
  transfers between devices with their start and end apart: 3, of which 3 were waited for; matrix products, arithmetic and copies ran while one was open for 2% of the time, Pallas kernels for 0%

profile of v1, /device:TPU:8, one launch (start us, length us, event | category | flops | bytes accessed | tf_op | source)
XLA Modules:
  0.0 316.2 jit_solution(17207909610854124284)
XLA Ops:
  6.5 0.0 copy-start
  6.5 0.0 copy-start.3
  6.5 0.0 all-reduce.3.cloned.1.call-start
  6.5 1.6 copy-done
  8.1 1.3 fusion.12
  9.4 0.9 add_dynamic-update-slice_fusion
  10.3 0.0 copy-start.2
  10.3 0.8 copy-done.2
  11.1 0.0 all-reduce.3.cloned.1.call-update
  11.1 0.0 all-gather.3.cloned.1.call-start
  11.2 0.0 copy-done.3
  11.2 0.1 copy.18
  11.3 0.1 eq.29
  11.4 0.1 eq.25
  11.6 0.1 copy.20
  11.7 0.2 fusion.5
  12.0 0.1 add_add_fusion
  12.0 0.1 copy.17
  12.1 0.1 mul.61
  12.3 0.1 reshape.100
  12.4 0.2 fusion.7
  12.7 2.9 scatter_custom_fusion
  15.6 53.9 %all-reduce.3.cloned.1.call-done = f32[64,2048]{1,0:T(8,128)} async-done(((f32[64,2048]{1,0:T(8,128)}), f32[64,2048]{1,0:T(8,128)}) %all-reduce.3.cloned.1.call-update) | async-done | bytes 524304 | tf_op jit(solution)/shard_map/psum | solution.py:31
  69.5 1.1 convert_element_type.27
  70.6 4.3 %gather_fusion = bf16[768,2048]{1,0:T(8,128)(2,1)} fusion(bf16[64,2048]{1,0:T(8,128)(2,1)S(1)} %convert_element_type.27, s32[1024]{0:T(1024)S(1)} %pad_clamp_fusion.1), kind=kCustom, calls=%fused_computation | custom fusion | bytes 6294528 | tf_op jit(solution)/shard_map/gather | solution.py:33
  74.9 6.3 %reshape.75 = bf16[128,6,2048]{2,1,0:T(8,128)(2,1)} reshape(bf16[768,2048]{1,0:T(8,128)(2,1)} %gather_fusion) | data formatting | bytes 6291456 | tf_op jit(solution)/shard_map/reshape | solution.py:33
  81.1 111.0 %all_to_all.10 = bf16[128,6,2048]{2,1,0:T(8,128)(2,1)} all-to-all(bf16[128,6,2048]{2,1,0:T(8,128)(2,1)} %reshape.75), channel_id=1, replica_groups=mesh['req'=128,'tp'=4] {'req'}, dimensions={0} | all-to-all | bytes 6291456 | tf_op jit(solution)/shard_map/all_to_all | solution.py:34
  192.1 6.3 %reshape.76 = bf16[768,2048]{1,0:T(8,128)(2,1)} reshape(bf16[128,6,2048]{2,1,0:T(8,128)(2,1)} %all_to_all.10) | data formatting | bytes 6291456 | tf_op jit(solution)/shard_map/reshape | solution.py:35
  198.4 0.0 copy-start.1
  198.4 0.0 copy-start.6
  198.4 3.3 %fusion.3 = f32[768,256]{1,0:T(8,128)S(1)} fusion(bf16[768,2048]{1,0:T(8,128)(2,1)} %reshape.76, bf16[1,2048,256]{2,1,0:T(8,128)(2,1)} %param.14), kind=kOutput, calls=%fused_computation.8 | convolution fusion | flops 805306368 | bytes 4980736 | tf_op jit(solution)/shard_map/dot_general | solution.py:36
  201.7 0.0 copy-done.1
  201.8 0.1 copy-done.6
  201.9 1.7 fusion
  203.6 0.0 all-gather.3.cloned.1.call-update
  203.6 38.7 %all-gather.3.cloned.1.call-done = bf16[768,1024]{1,0:T(8,128)(2,1)} async-done(((bf16[768,256]{1,0:T(8,128)(2,1)}), bf16[768,1024]{1,0:T(8,128)(2,1)}) %all-gather.3.cloned.1.call-update) | async-done | bytes 1572880 | tf_op jit(solution)/shard_map/all_gather | solution.py:40
  242.3 2.7 convolution_convert_fusion
  245.0 0.0 copy-start.4
  245.0 1.3 reshape.77
  246.3 14.6 %all-to-all-start.1 = ((bf16[128,6,512]{2,1,0:T(8,128)(2,1)}), bf16[128,6,512]{2,1,0:T(8,128)(2,1)}, u32[]{:S(2)}, u32[]{:S(2)}) async-start(bf16[128,6,512]{2,1,0:T(8,128)(2,1)} %reshape.77), calls=%async_computation.1 | async-start | bytes 2097152 | tf_op jit(solution)/shard_map/all_to_all | solution.py:45
  260.9 0.0 copy-done.4
  260.9 0.7 copy.22
  261.6 1.3 dynamic-slice
  263.5 28.3 %all-to-all-done.1 = bf16[128,6,512]{2,1,0:T(8,128)(2,1)} async-done(((bf16[128,6,512]{2,1,0:T(8,128)(2,1)}), bf16[128,6,512]{2,1,0:T(8,128)(2,1)}, u32[]{:S(2)}, u32[]{:S(2)}) %all-to-all-start.1) | async-done | bytes 786464 | tf_op jit(solution)/shard_map/all_to_all | solution.py:45
  291.9 1.4 reshape.78
  293.2 0.0 copy-start.5
  293.3 2.1 gather_fusion.1
  295.3 0.1 reshape.79
  295.4 1.1 multiply_reduce_fusion
  296.6 1.0 multiply_reduce_fusion.1
  297.6 0.2 dynamic-update-slice
  297.9 9.8 %all-reduce = f32[256]{0:T(256)S(1)} all-reduce(f32[256]{0:T(256)S(1)} %dynamic-update-slice), channel_id=2, replica_groups=mesh['req'=128,'tp'=4] {'tp'}, use_global_device_ids=true, to_apply=%add | all-reduce | flops 256 | bytes 2048
  307.6 0.1 reshape.104
  307.8 0.0 copy-done.5
  307.8 1.6 multiply_convert_fusion
  (12 shorter events, 0.1 us)
Async XLA Ops:
  6.5 1.6 copy-start
  6.5 4.6 %copy-start.3 = (s32[64,6]{0,1:T(8,128)S(1)}, s32[64,6]{0,1:T(8,128)}, u32[]{:S(2)}) copy-start(s32[64,6]{0,1:T(8,128)} %param.12) | copy-start | bytes 4612
  6.5 63.0 %all-reduce.3.cloned.1.call-start = ((), (), s32[]{:S(2)}) async-start(), calls=%async_computation.2 | async-start | bytes 1048576 | tf_op jit(solution)/shard_map/psum | solution.py:31
  10.3 0.8 copy-start.2
  11.1 231.1 %all-gather.3.cloned.1.call-start = ((), (), s32[]{:S(2)}) async-start(), calls=%async_computation.3 | async-start | bytes 1966080 | tf_op jit(solution)/shard_map/all_gather | solution.py:40
  198.4 3.3 %copy-start.1 = (bf16[768,2048]{1,0:T(8,128)(2,1)S(1)}, bf16[768,2048]{1,0:T(8,128)(2,1)}, u32[]{:S(2)}) copy-start(bf16[768,2048]{1,0:T(8,128)(2,1)} %reshape.76) | copy-start | bytes 9437188
  198.4 3.4 %copy-start.6 = (bf16[1,2048,256]{2,1,0:T(8,128)(2,1)S(1)}, bf16[1,2048,256]{2,1,0:T(8,128)(2,1)}, u32[]{:S(2)}) copy-start(bf16[1,2048,256]{2,1,0:T(8,128)(2,1)} %param.15) | copy-start | bytes 3145732
  245.0 15.9 %copy-start.4 = (f32[64,6]{0,1:T(8,128)S(1)}, f32[64,6]{0,1:T(8,128)}, u32[]{:S(2)}) copy-start(f32[64,6]{0,1:T(8,128)} %param.13) | copy-start | bytes 4612
  246.3 45.6 %all-to-all-start.1 = ((bf16[128,6,512]{2,1,0:T(8,128)(2,1)}), bf16[128,6,512]{2,1,0:T(8,128)(2,1)}, u32[]{:S(2)}, u32[]{:S(2)}) async-start(bf16[128,6,512]{2,1,0:T(8,128)(2,1)} %reshape.77), calls=%async_computation.1 | async-start | bytes 2097152 | tf_op jit(solution)/shard_map/all_to_all | solution.py:45
  293.2 14.5 %copy-start.5 = (f32[512]{0:T(512)S(1)}, f32[512]{0:T(512)}, u32[]{:S(2)}) copy-start(f32[512]{0:T(512)} %param.17) | copy-start | bytes 6148
Sparse Core Ops, SparseCore 0:
  11.3 58.2 all-reduce.2
  203.7 38.5 all-gather.2
